TPU v7x, 128 devices: a whole 4x4x4 slice. The times are simulated.
128 devices in a mesh: grp: 2 (over y_lo), row: 16 (over x, z), hid: 4 (over y_hi, core).
Axes of the slice: x: 4, y: 4 (y_hi: 2, y_lo: 2; y = y_hi * 2 + y_lo), z: 4, core: 2. Of those that a mesh axis runs over, the one named last changes fastest.
Arguments:
- token_ids: int32 [512, 64], P(('grp', 'row')), may hold values from 0 to 128255, as said below
- activations: bfloat16 [512, 64, 4096], P(('grp', 'row'), None, 'hid'), may hold values from -6 to 6
- out_grads: bfloat16 [512, 64, 4096], P(('grp', 'row'), None, 'hid'), may hold values from -6 to 6
- proj_in: bfloat16 [64, 4096], P(None, 'hid'), may hold values from -0.09375 to 0.09375
- proj_out: bfloat16 [64, 4096], P(None, 'hid'), may hold values from -0.09375 to 0.09375
- inverse_curvature: float32 [4096, 4096], P('row', ('grp', 'hid')), as said below
- store_grads: bfloat16 [262144, 4096], P(('grp', 'row', 'hid')), may hold values from -1 to 1
- store_order: int32 [262144], P(('grp', 'row', 'hid')), may hold values from 0 to 262143, each once
- example_ids: int32 [512], replicated, may hold values from 0 to 262143
Outputs:
- scores: bfloat16 [262144, 512], P(('grp', 'row', 'hid'))
Inputs may be any that keep to these rules, and one draw needn't show every extreme that they name: `token_ids`: 0 marks padding, which only follows a query's tokens; each query has at least 16 tokens that are not padding. `example_ids`: each query's id names a stored example. `inverse_curvature`: symmetric.
All inputs are finite; a program needn't handle non-finite values.
Results may differ from a plain program's by a relative error of at most 0.013.
Values may be sent and summed in bfloat16 or wider, within the bound.
No kernel may reach another device: no remote copies, remote signals or barrier semaphores. Data moves between devices by JAX's collectives and lax.ppermute only.
A program may use at most 128 MiB of HBM per device.

v0:
```python
import jax
import jax.numpy as jnp
from jax import lax
from jax.sharding import PartitionSpec as P


def copy_for_each(value, axis):
    devices = lax.axis_size(axis)
    return lax.all_to_all(
        jnp.broadcast_to(value[None], (devices, *value.shape)), axis, 0, 0, tiled=True
    )


def over_copies(value, axis):
    everything = copy_for_each(value, axis)
    return jnp.sum(everything, axis=0)


def laid_out(blocks, dim):
    blocks = jnp.moveaxis(blocks, 0, dim)
    lengths = blocks.shape
    return blocks.reshape(*lengths[:dim], lengths[dim] * lengths[dim + 1], *lengths[dim + 2 :])


def collect(value, axis, dim):
    return laid_out(copy_for_each(value, axis), dim)


def in_blocks(value, dim, devices):
    before, after = (value.shape[:dim], value.shape[dim + 1 :])
    return jnp.moveaxis(value.reshape(*before, devices, -1, *after), dim, 0)


def sent_and_summed(value, axis, dim):
    blocks = in_blocks(value, dim, lax.axis_size(axis))
    arrived = lax.all_to_all(blocks, axis, split_axis=0, concat_axis=0, tiled=True)
    return arrived.sum(axis=0)


def local(
    token_ids,
    activations,
    out_grads,
    proj_in,
    proj_out,
    inverse_curvature,
    store_grads,
    store_order,
    example_ids,
):
    queries_here, query_tokens, width_here = activations.shape
    rank_side = proj_in.shape[0]
    contract = (((1,), (1,)), ((), ()))
    flat_inputs = activations.reshape(queries_here * query_tokens, width_here)
    flat_grads = out_grads.reshape(queries_here * query_tokens, width_here)
    out_part = lax.dot_general(flat_grads, proj_out, contract, preferred_element_type=jnp.float32)
    in_part = lax.dot_general(flat_inputs, proj_in, contract, preferred_element_type=jnp.float32)
    projected = jnp.concatenate([out_part, in_part], axis=1)
    projected = over_copies(projected, "hid")
    out_side = projected[:, :rank_side].reshape(queries_here, query_tokens, rank_side)
    in_side = projected[:, rank_side:].reshape(queries_here, query_tokens, rank_side)
    usable = (token_ids > 0).astype(jnp.float32)
    counted = jnp.sum(usable, axis=1, keepdims=True)
    weights = usable / counted
    scaled = out_side * weights[:, :, None]
    query_grads = jnp.einsum("qla,qlb->qab", scaled, in_side).reshape(
        queries_here, rank_side * rank_side
    )
    query_block = lax.all_to_all(query_grads, "row", split_axis=1, concat_axis=0, tiled=True)
    query_block = collect(query_block, "grp", 0)
    partial_value = jnp.dot(
        query_block,
        inverse_curvature,
        precision=lax.Precision.HIGHEST,
        preferred_element_type=jnp.float32,
    )
    pre_share = sent_and_summed(partial_value, "row", 0).astype(jnp.bfloat16)
    pre_share = collect(pre_share, ("grp", "hid"), 1)
    scores = lax.dot_general(
        store_grads,
        lax.all_gather(pre_share, "row", axis=0, tiled=True),
        contract,
        preferred_element_type=jnp.float32,
    )
    is_self = store_order[:, None] == example_ids[None, :]
    return jnp.where(is_self, 0.0, scores).astype(jnp.bfloat16)


def solution(mesh):
    placed = (
        P(("grp", "row"), None),
        P(("grp", "row"), None, "hid"),
        P(("grp", "row"), None, "hid"),
        P(None, "hid"),
        P(None, "hid"),
        P("row", ("grp", "hid")),
        P(("grp", "row", "hid"), None),
        P(("grp", "row", "hid")),
        P(),
    )
    return jax.shard_map(
        local, mesh=mesh, in_specs=placed, out_specs=P(("grp", "row", "hid"), None), check_vma=False
    )
```

profile of v0, /device:TPU:1, one launch (start us, length us, event | category | flops | bytes accessed | tf_op | source)
XLA Modules:
  0.0 177.7 jit_solution(14987090511426984861)
XLA Ops:
  6.5 0.0 copy-start
  6.5 1.6 copy-done
  8.1 1.7 fusion.6
  9.8 2.4 %fusion.5 = f32[1024,64]{0,1:T(8,128)S(1)} fusion(bf16[1024,1024]{1,0:T(8,128)(2,1)} %bitcast.29, bf16[64,1024]{1,0:T(8,128)(2,1)} %param.13), kind=kOutput, calls=%fused_computation.11 | convolution fusion | flops 134217728 | bytes 2490368 | tf_op jit(solution)/shard_map/dot_general | solution.py:56
  12.2 0.0 copy-start.2
  12.2 0.2 copy.23
  12.4 1.5 broadcast_in_dim.12
  13.9 6.0 %all-to-all-start = ((f32[4,1024,128]{2,1,0:T(8,128)}), f32[4,1024,128]{2,1,0:T(8,128)}, u32[]{:S(2)}, u32[]{:S(2)}) async-start(f32[4,1024,128]{2,1,0:T(8,128)} %broadcast_in_dim.12), calls=%async_computation | async-start | bytes 4194304 | tf_op jit(solution)/shard_map/all_to_all | solution.py:9
  19.8 0.0 all-gather.2.cloned.1.call-start
  19.8 0.0 copy-done.2
  19.8 0.1 convert_reduce_fusion
  19.9 0.1 convert_divide_fusion
  20.0 26.1 %all-to-all-done = f32[4,1024,128]{2,1,0:T(8,128)} async-done(((f32[4,1024,128]{2,1,0:T(8,128)}), f32[4,1024,128]{2,1,0:T(8,128)}, u32[]{:S(2)}, u32[]{:S(2)}) %all-to-all-start) | async-done | bytes 2097184 | tf_op jit(solution)/shard_map/all_to_all | solution.py:9
  46.1 1.8 reduce_sum.27
  47.9 0.1 slice.9
  48.0 0.3 copy.29
  48.4 0.0 copy-start.1
  48.4 0.2 fusion.3
  48.6 0.2 all_to_all.25
  48.8 0.2 copy.26
  48.9 14.9 %all_to_all.36 = f32[16,16,256]{2,0,1:T(8,128)S(1)} all-to-all(f32[16,16,256]{2,0,1:T(8,128)S(1)} %copy.26), channel_id=1, replica_groups=mesh['grp'=2,'row'=16,'hid'=4] {'row'}, dimensions={1} | all-to-all | bytes 524288 | tf_op jit(solution)/shard_map/all_to_all | solution.py:69
  63.8 7.8 %all_to_all.37 = f32[2,256,256]{2,1,0:T(8,128)S(1)} all-to-all(f32[2,256,256]{2,1,0:T(8,128)S(1)} %broadcast_in_dim.14), channel_id=1, replica_groups=mesh['grp'=2,'row'=16,'hid'=4] {'grp'}, dimensions={0} | all-to-all | bytes 1048576 | tf_op jit(solution)/shard_map/all_to_all | solution.py:9
  71.7 0.0 copy-done.1
  71.7 1.0 fusion.1
  72.7 17.1 %all_to_all.38 = f32[16,32,512]{2,1,0:T(8,128)S(1)} all-to-all(f32[16,32,512]{2,1,0:T(8,128)S(1)} %fusion.1), channel_id=1, replica_groups=mesh['grp'=2,'row'=16,'hid'=4] {'row'}, dimensions={0} | all-to-all | bytes 2097152 | tf_op jit(solution)/shard_map/all_to_all | solution.py:36
  89.8 0.1 reduce_sum.29
  89.9 13.6 %all_to_all.39 = bf16[8,32,512]{2,1,0:T(8,128)(2,1)S(1)} all-to-all(bf16[8,32,512]{2,1,0:T(8,128)(2,1)S(1)} %broadcast_in_dim.15), channel_id=1, replica_groups=mesh['grp'=2,'row'=16,'hid'=4] {'grp','hid'}, dimensions={0} | all-to-all | bytes 524288 | tf_op jit(solution)/shard_map/all_to_all | solution.py:9
  103.5 0.7 copy.30
  104.3 0.0 all-gather.2.cloned.1.call-update
  104.3 48.0 %all-gather.2.cloned.1.call-done = bf16[512,4096]{1,0:T(8,128)(2,1)} async-done(((bf16[32,4096]{1,0:T(8,128)(2,1)}), bf16[512,4096]{1,0:T(8,128)(2,1)}) %all-gather.2.cloned.1.call-update) | async-done | bytes 4194320 | tf_op jit(solution)/shard_map/all_gather | solution.py:81
  152.3 14.7 %fusion = bf16[2048,512]{0,1:T(8,128)(2,1)} fusion(bf16[512,4096]{1,0:T(8,128)(2,1)} %all-gather.2.cloned.1.call-done, bf16[2048,4096]{1,0:T(8,128)(2,1)} %param.15, s32[2048]{0:T(1024)S(1)} %copy-done.3, s32[512]{0:T(512)S(1)} %copy-done.4), kind=kOutput, calls=%fused_computation.1 | convolution fusion | flops 8593080320 | bytes 23078912 | tf_op jit(solution)/shard_map/dot_general | solution.py:79
  166.9 3.9 %copy.28 = bf16[2048,512]{1,0:T(8,128)(2,1)} copy(bf16[2048,512]{0,1:T(8,128)(2,1)} %fusion) | data formatting | bytes 4194304 | tf_op jit(solution)/shard_map/convert_element_type | solution.py:86
  (8 shorter events, 0.1 us)
Async XLA Ops:
  6.5 1.6 copy-start
  12.2 7.6 %copy-start.2 = (s32[16,64]{1,0:T(8,128)S(1)}, s32[16,64]{1,0:T(8,128)}, u32[]{:S(2)}) copy-start(s32[16,64]{1,0:T(8,128)} %param.9) | copy-start | bytes 12292
  13.9 32.3 %all-to-all-start = ((f32[4,1024,128]{2,1,0:T(8,128)}), f32[4,1024,128]{2,1,0:T(8,128)}, u32[]{:S(2)}, u32[]{:S(2)}) async-start(f32[4,1024,128]{2,1,0:T(8,128)} %broadcast_in_dim.12), calls=%async_computation | async-start | bytes 4194304 | tf_op jit(solution)/shard_map/all_to_all | solution.py:9
  19.8 132.4 %all-gather.2.cloned.1.call-start = ((), (), s32[]{:S(2)}) async-start(), calls=%async_computation.5 | async-start | bytes 4456448 | tf_op jit(solution)/shard_map/all_gather | solution.py:81
  48.4 23.3 %copy-start.1 = (f32[256,512]{1,0:T(8,128)S(1)}, f32[256,512]{1,0:T(8,128)}, u32[]{:S(2)}) copy-start(f32[256,512]{1,0:T(8,128)} %param.14) | copy-start | bytes 1572868
  63.8 88.4 %copy-start.3 = (s32[2048]{0:T(1024)S(1)}, s32[2048]{0:T(1024)}, u32[]{:S(2)}) copy-start(s32[2048]{0:T(1024)} %param.16) | copy-start | bytes 24580
  63.8 88.4 %copy-start.4 = (s32[512]{0:T(512)S(1)}, s32[512]{0:T(512)}, u32[]{:S(2)}) copy-start(s32[512]{0:T(512)} %param.17) | copy-start | bytes 6148
Sparse Core Ops, SparseCore 0:
  104.4 47.7 all-gather.1
where the time goes:
time: 178 us
  waiting for transfers between devices  74.1 us (42%)
  blocking collectives  53.4 us (30%)
  matrix products  19.9 us (11%)
  between operations  13.5 us (8%)
  local copies, waits for them, and re-layouts  8.71 us (5%)
  starting transfers between devices  5.96 us (3%)
  other arithmetic  2.11 us (1%)
    all_gather x1, waiting for transfers between devices, local(): lax.all_gather(pre_share, 'row', axis=0, tiled=True)  48 us
    all_to_all x1, waiting for transfers between devices, copy_for_each(): lax.all_to_all(jnp.broadcast_to(value[None], (devices, *value.shape)), ax...  26.1 us
    all_to_all x2, blocking collectives, copy_for_each(): lax.all_to_all(jnp.broadcast_to(value[None], (devices, *value.shape)), ax...  21.5 us
    all_to_all x1, blocking collectives, sent_and_summed(): lax.all_to_all(blocks, axis, split_axis=0, concat_axis=0, tiled=True)  17.1 us
    all_to_all x1, blocking collectives, local(): lax.all_to_all(query_grads, 'row', split_axis=1, concat_axis=0, tiled=True)  14.9 us
    dot_general x1, matrix products, local(): lax.dot_general(store_grads, lax.all_gather(pre_share, 'row', axis=0, til...  14.7 us
    all_to_all x1, starting transfers between devices, copy_for_each(): lax.all_to_all(jnp.broadcast_to(value[None], (devices, *value.shape)), ax...  5.95 us
    convert_element_type x1, local copies, waits for them, and re-layouts, local(): return jnp.where(is_self, 0.0, scores).astype(jnp.bfloat16)  3.92 us
  transfers between devices with their start and end apart: 2, of which 2 were waited for; matrix products, arithmetic and copies ran while one was open for 0% of the time, Pallas kernels for 0%

commit v1 on v0

--- a/solution.py
+++ b/solution.py
@@ -2,6 +2,11 @@
 import jax.numpy as jnp
 from jax import lax
 from jax.sharding import PartitionSpec as P
+
+
+def swapped_in(x, axis, dim):
+    repeated = jnp.stack([x] * lax.axis_size(axis))
+    return jnp.concatenate(lax.all_to_all(repeated, axis, 0, 0), axis=dim)
 
 
 def copy_for_each(value, axis):
@@ -77,10 +82,7 @@
     pre_share = sent_and_summed(partial_value, "row", 0).astype(jnp.bfloat16)
     pre_share = collect(pre_share, ("grp", "hid"), 1)
     scores = lax.dot_general(
-        store_grads,
-        lax.all_gather(pre_share, "row", axis=0, tiled=True),
-        contract,
-        preferred_element_type=jnp.float32,
+        store_grads, swapped_in(pre_share, "row", 0), contract, preferred_element_type=jnp.float32
     )
     is_self = store_order[:, None] == example_ids[None, :]
     return jnp.where(is_self, 0.0, scores).astype(jnp.bfloat16)

time: 178 us -> 169 us (0.949)
  blocking collectives: 53.4 us -> 106 us
  waiting for transfers between devices: 74.1 us -> 26.1 us
  between operations: 13.5 us -> 0.13 us
    all_to_all x0 -> x1, blocking collectives: none -> 52.7 us  [swapped_in(): return jnp.concatenate(lax.all_to_all(repeated, axis, 0, 0), axis=dim)]
    all_gather x1 -> x0, waiting for transfers between devices: 48 us -> none  [local(): lax.all_gather(pre_share, 'row', axis=0, tiled=True)]
  transfers between devices with their start and end apart: 2 -> 1, of which waited for: 2 -> 1; matrix products, arithmetic and copies ran while one was open for 0% -> 0% of each run, Pallas kernels for 0% -> 0%
where the time goes in v1:
time: 169 us; the launch traced here: 168 us
  blocking collectives  106 us (63%)
  waiting for transfers between devices  26.1 us (15%)
  matrix products  18.7 us (11%)
  local copies, waits for them, and re-layouts  8.5 us (5%)
  starting transfers between devices  5.95 us (4%)
  other arithmetic  2.11 us (1%)
    all_to_all x1, blocking collectives, swapped_in(): return jnp.concatenate(lax.all_to_all(repeated, axis, 0, 0), axis=dim)  52.7 us
    all_to_all x1, waiting for transfers between devices, copy_for_each(): lax.all_to_all(jnp.broadcast_to(value[None], (devices, *value.shape)), ax...  26.1 us
    all_to_all x2, blocking collectives, copy_for_each(): lax.all_to_all(jnp.broadcast_to(value[None], (devices, *value.shape)), ax...  21.5 us
    all_to_all x1, blocking collectives, sent_and_summed(): lax.all_to_all(blocks, axis, split_axis=0, concat_axis=0, tiled=True)  17.1 us
    all_to_all x1, blocking collectives, local(): lax.all_to_all(query_grads, 'row', split_axis=1, concat_axis=0, tiled=True)  14.9 us
    dot_general x1, matrix products, local(): lax.dot_general(store_grads, swapped_in(pre_share, 'row', 0), contract, p...  13.5 us
    all_to_all x1, starting transfers between devices, copy_for_each(): lax.all_to_all(jnp.broadcast_to(value[None], (devices, *value.shape)), ax...  5.95 us
    convert_element_type x1, local copies, waits for them, and re-layouts, local(): return jnp.where(is_self, 0.0, scores).astype(jnp.bfloat16)  3.92 us
  transfers between devices with their start and end apart: 1, of which 1 were waited for; matrix products, arithmetic and copies ran while one was open for 0% of the time, Pallas kernels for 0%

profile of v1, /device:TPU:1, one launch (start us, length us, event | category | flops | bytes accessed | tf_op | source)
XLA Modules:
  0.0 167.6 jit_solution(13074667267413160068)
XLA Ops:
  0.0 0.0 copy-start
  0.0 1.6 copy-done
  1.6 1.7 fusion.6
  3.3 2.4 %fusion.5 = f32[1024,64]{0,1:T(8,128)S(1)} fusion(bf16[1024,1024]{1,0:T(8,128)(2,1)} %bitcast.31, bf16[64,1024]{1,0:T(8,128)(2,1)} %param.13), kind=kOutput, calls=%fused_computation.11 | convolution fusion | flops 134217728 | bytes 2490368 | tf_op jit(solution)/shard_map/dot_general | solution.py:61
  5.7 0.0 copy-start.2
  5.7 0.2 copy.23
  5.9 1.5 broadcast_in_dim.12
  7.3 6.0 %all-to-all-start = ((f32[4,1024,128]{2,1,0:T(8,128)}), f32[4,1024,128]{2,1,0:T(8,128)}, u32[]{:S(2)}, u32[]{:S(2)}) async-start(f32[4,1024,128]{2,1,0:T(8,128)} %broadcast_in_dim.12), calls=%async_computation | async-start | bytes 4194304 | tf_op jit(solution)/shard_map/all_to_all | solution.py:14
  13.3 0.1 convert_reduce_fusion
  13.4 0.1 convert_divide_fusion
  13.5 26.1 %all-to-all-done = f32[4,1024,128]{2,1,0:T(8,128)} async-done(((f32[4,1024,128]{2,1,0:T(8,128)}), f32[4,1024,128]{2,1,0:T(8,128)}, u32[]{:S(2)}, u32[]{:S(2)}) %all-to-all-start) | async-done | bytes 2097184 | tf_op jit(solution)/shard_map/all_to_all | solution.py:14
  39.6 1.8 %reduce_sum.27 = f32[1024,128]{1,0:T(8,128)S(1)} reduce(f32[4,1024,128]{2,1,0:T(8,128)} %all-to-all-done, f32[]{:T(128)} %constant.0.clone.1), dimensions={0}, to_apply=%region_0.0 | reduce | flops 393216 | bytes 2621444 | tf_op jit(solution)/shard_map/reduce_sum | solution.py:21
  41.4 0.1 slice.9
  41.5 0.3 copy.29
  41.8 0.0 copy-start.1
  41.8 0.2 fusion.3
  42.1 0.2 all_to_all.28
  42.2 0.2 copy.26
  42.4 14.9 %all_to_all.41 = f32[16,16,256]{2,0,1:T(8,128)S(1)} all-to-all(f32[16,16,256]{2,0,1:T(8,128)S(1)} %copy.26), channel_id=1, replica_groups=mesh['grp'=2,'row'=16,'hid'=4] {'row'}, dimensions={1} | all-to-all | bytes 524288 | tf_op jit(solution)/shard_map/all_to_all | solution.py:74
  57.3 7.8 %all_to_all.42 = f32[2,256,256]{2,1,0:T(8,128)S(1)} all-to-all(f32[2,256,256]{2,1,0:T(8,128)S(1)} %broadcast_in_dim.14), channel_id=1, replica_groups=mesh['grp'=2,'row'=16,'hid'=4] {'grp'}, dimensions={0} | all-to-all | bytes 1048576 | tf_op jit(solution)/shard_map/all_to_all | solution.py:14
  65.2 0.0 copy-done.1
  65.2 1.0 fusion.1
  66.2 17.1 %all_to_all.43 = f32[16,32,512]{2,1,0:T(8,128)S(1)} all-to-all(f32[16,32,512]{2,1,0:T(8,128)S(1)} %fusion.1), channel_id=1, replica_groups=mesh['grp'=2,'row'=16,'hid'=4] {'row'}, dimensions={0} | all-to-all | bytes 2097152 | tf_op jit(solution)/shard_map/all_to_all | solution.py:41
  83.3 0.1 reduce_sum.29
  83.4 13.6 %all_to_all.44 = bf16[8,32,512]{2,1,0:T(8,128)(2,1)S(1)} all-to-all(bf16[8,32,512]{2,1,0:T(8,128)(2,1)S(1)} %broadcast_in_dim.15), channel_id=1, replica_groups=mesh['grp'=2,'row'=16,'hid'=4] {'grp','hid'}, dimensions={0} | all-to-all | bytes 524288 | tf_op jit(solution)/shard_map/all_to_all | solution.py:14
  97.0 0.5 stack.3
  97.5 0.0 copy-start.3
  97.5 0.0 copy-start.4
  97.6 52.7 %all_to_all.45 = bf16[16,32,4096]{2,1,0:T(8,128)(2,1)S(1)} all-to-all(bf16[16,32,4096]{2,1,0:T(8,128)(2,1)S(1)} %stack.3), channel_id=1, replica_groups=mesh['grp'=2,'row'=16,'hid'=4] {'row'}, dimensions={0} | all-to-all | bytes 8388608 | tf_op jit(solution)/shard_map/all_to_all | solution.py:9
  150.2 0.0 copy-done.3
  150.3 13.5 %fusion = bf16[2048,512]{0,1:T(8,128)(2,1)} fusion(bf16[512,4096]{1,0:T(8,128)(2,1)S(1)} %bitcast.29, bf16[2048,4096]{1,0:T(8,128)(2,1)} %param.15, s32[2048]{0:T(1024)S(1)} %copy-done.3, s32[512]{0:T(512)S(1)} %copy-done.4), kind=kOutput, calls=%fused_computation.1 | convolution fusion | flops 8593080320 | bytes 23078912 | tf_op jit(solution)/shard_map/dot_general | solution.py:84
  163.7 3.9 %copy.28 = bf16[2048,512]{1,0:T(8,128)(2,1)} copy(bf16[2048,512]{0,1:T(8,128)(2,1)} %fusion) | data formatting | bytes 4194304 | tf_op jit(solution)/shard_map/convert_element_type | solution.py:88
  (7 shorter events, 0.2 us)
Async XLA Ops:
  0.0 1.6 copy-start
  5.7 7.6 %copy-start.2 = (s32[16,64]{1,0:T(8,128)S(1)}, s32[16,64]{1,0:T(8,128)}, u32[]{:S(2)}) copy-start(s32[16,64]{1,0:T(8,128)} %param.9) | copy-start | bytes 12292
  7.3 32.3 %all-to-all-start = ((f32[4,1024,128]{2,1,0:T(8,128)}), f32[4,1024,128]{2,1,0:T(8,128)}, u32[]{:S(2)}, u32[]{:S(2)}) async-start(f32[4,1024,128]{2,1,0:T(8,128)} %broadcast_in_dim.12), calls=%async_computation | async-start | bytes 4194304 | tf_op jit(solution)/shard_map/all_to_all | solution.py:14
  41.8 23.3 %copy-start.1 = (f32[256,512]{1,0:T(8,128)S(1)}, f32[256,512]{1,0:T(8,128)}, u32[]{:S(2)}) copy-start(f32[256,512]{1,0:T(8,128)} %param.14) | copy-start | bytes 1572868
  97.5 52.7 %copy-start.3 = (s32[2048]{0:T(1024)S(1)}, s32[2048]{0:T(1024)}, u32[]{:S(2)}) copy-start(s32[2048]{0:T(1024)} %param.16) | copy-start | bytes 24580
  97.5 52.7 %copy-start.4 = (s32[512]{0:T(512)S(1)}, s32[512]{0:T(512)}, u32[]{:S(2)}) copy-start(s32[512]{0:T(512)} %param.17) | copy-start | bytes 6148
